TPU v7x, 32 devices: a whole 2x2x4 slice. The times are simulated.
32 devices in a mesh: lon: 8 (over y, x, core), lat: 4 (over z).
Axes of the slice: x: 2, y: 2, z: 4, core: 2. Of those that a mesh axis runs over, the one named last changes fastest.
Arguments:
- tokens: bfloat16 [6, 288, 192, 192], P(None, 'lat', 'lon'), may hold values from -6 to 6
- obs_values: bfloat16 [65536, 256], P(('lon', 'lat')), may hold values from -6 to 6
- obs_dest: int32 [65536], P(('lon', 'lat')), may hold values from 0 to 31, as said below
- obs_cell: int32 [65536], P(('lon', 'lat')), may hold values from 0 to 10367
- obs_count: int32 [32], P(('lon', 'lat')), may hold values from 1365 to 2048, as said below
- w_obs: bfloat16 [256, 192], replicated, may hold values from -0.375 to 0.375
- ln1_gain: float32 [192], replicated, may hold values from 0.1 to 1.9
- w_qkv: bfloat16 [192, 576], replicated, may hold values from -0.4375 to 0.4375
- position_bias: float32 [6, 144, 144], replicated, may hold values from -4 to 400
- w_proj: bfloat16 [192, 192], replicated, may hold values from -0.4375 to 0.4375
- ln2_gain: float32 [192], replicated, may hold values from 0.1 to 1.9
- w_up: bfloat16 [192, 768], replicated, may hold values from -0.4375 to 0.4375
- w_down: bfloat16 [768, 192], replicated, may hold values from -0.21875 to 0.21875
Outputs:
- block_out: bfloat16 [6, 288, 192, 192], P(None, 'lat', 'lon')
Inputs may be any that keep to these rules, and one draw needn't show every extreme that they name: `obs_dest`: the tile owning a row, numbered lon index * 4 + lat index; among the live rows of one device no tile is named more than 128 times, and in every draw one tile is named exactly 128 times by the live rows of every device. `obs_cell`: a cell of the owning tile, numbered (level * 72 + row) * 24 + column. The live rows of device s are the first obs_count[s] rows of its block; the others are padding.
All inputs are finite; a program needn't handle non-finite values.
Results may differ from a plain program's by a relative error of at most 0.01.
Values may be sent and summed in bfloat16 or wider, within the bound.
No kernel may reach another device: no remote copies, remote signals or barrier semaphores. Data moves between devices by JAX's collectives and lax.ppermute only.
A program may use at most 128 MiB of HBM per device.

v0:
```python
import functools
import math

import jax
import jax.numpy as jnp
from jax import lax
from jax.experimental import pallas as pl
from jax.experimental.pallas import tpu as pltpu
from jax.sharding import PartitionSpec as P

WZ = 2
WLAT = 6
WLON = 12

NT = (((1,), (1,)), ((), ()))
TN = (((0,), (0,)), ((), ()))


def layer_norm(x, gain):
    n = x.shape[-1]
    mean = jnp.sum(x, axis=-1, keepdims=True) * (1.0 / n)
    c = x - mean
    var = jnp.sum(c * c, axis=-1, keepdims=True) * (1.0 / n)
    return c * lax.rsqrt(var + 1e-5) * gain


def dot(a, b):
    return jnp.dot(a, b, preferred_element_type=jnp.float32)


def attend_all(xs, tabs, g1, wk, wqv, wproj, heads, lag=1):
    bf, f32 = jnp.bfloat16, jnp.float32
    win, d = xs[0].shape
    hd, tail = d // heads, win - 128
    reps, n = 128 // tail, len(xs)
    nx = [layer_norm(x, g1).astype(bf) for x in xs]
    kk, q, v = [], [], []
    for i in range(n):
        kk.append(dot(nx[i], wk).astype(bf))
        ext = jnp.concatenate([nx[i][:128]] + [nx[i][128:]] * reps, axis=0)
        qv = lax.dot_general(wqv, ext, NT, preferred_element_type=f32)
        q.append((qv[:d] * (math.log2(math.e) / math.sqrt(hd))).astype(bf))
        v.append(qv[d:].astype(bf)[:, :win])
    ones = jnp.ones((16, win), bf)
    zero = jnp.zeros((hd, 128), bf)
    mask = (lax.broadcasted_iota(jnp.int32, (d, 128), 0) // hd) == (lax.broadcasted_iota(jnp.int32, (d, 128), 1) // tail)
    jobs = [(i, p) for i in range(n) for p in range(heads // 2 + 1)]
    s_of, e_of, c_of = {}, {}, {}

    def scores(i, p):
        if p < heads // 2:
            cols = [jnp.concatenate([q[i][hd * h:hd * h + hd, :128] if j == h else zero for j in range(heads)], axis=0)
                    for h in (2 * p, 2 * p + 1)]
            rhs = jnp.concatenate(cols, axis=1)
        else:
            rhs = jnp.where(mask, q[i][:, 128:].astype(f32), 0.0).astype(bf)
        s_of[i, p] = dot(kk[i], rhs) + tabs[i][:, 256 * p:256 * p + rhs.shape[1]]

    def soft(i, p):
        s = s_of.pop((i, p))
        e_of[i, p] = jnp.exp2(s - jnp.max(s, axis=0, keepdims=True)).astype(bf)

    def values(i, p):
        e = e_of.pop((i, p))
        if p < heads // 2:
            o = dot(jnp.concatenate([v[i][2 * hd * p:2 * hd * p + 2 * hd], ones], axis=0), e)
            r = 1.0 / o[2 * hd:2 * hd + 1]
            c_of[i, p] = [(o[:hd, :128] * r[:, :128]).astype(bf), (o[hd:2 * hd, 128:] * r[:, 128:]).astype(bf)]
        else:
            o = dot(jnp.concatenate([v[i], ones], axis=0), e)
            c_of[i, p] = jnp.where(mask, o[:d] * (1.0 / o[d:d + 1]), 0.0).astype(bf)

    ys = []
    def finish(i):
        main = jnp.concatenate([c for p in range(heads // 2) for c in c_of[i, p]], axis=0)
        ctx = jnp.concatenate([main, c_of[i, heads // 2]], axis=1)
        proj = lax.dot_general(ctx, wproj, TN, preferred_element_type=f32)
        fold = proj[128:128 + tail]
        for h in range(1, heads):
            fold = fold + proj[128 + tail * h:128 + tail * h + tail]
        ys.append((xs[i] + jnp.concatenate([proj[:128], fold], axis=0)).astype(bf))

    for t in range(len(jobs) + 2 * lag):
        if t < len(jobs):
            scores(*jobs[t])
        if 0 <= t - lag < len(jobs):
            soft(*jobs[t - lag])
        if 0 <= t - 2 * lag < len(jobs):
            values(*jobs[t - 2 * lag])
            if jobs[t - 2 * lag][1] == heads // 2:
                finish(jobs[t - 2 * lag][0])
    return ys


def ffn_all(ys, g2, wup, wdown):
    bf = jnp.bfloat16
    n2 = [layer_norm(y.astype(jnp.float32), g2).astype(bf) for y in ys]
    outs = []
    for i in range(len(ys)):
        u = dot(n2[i], wup)
        h = (0.5 * u * (1.0 + lax.erf(u * (1.0 / math.sqrt(2.0))))).astype(bf)
        outs.append((ys[i].astype(jnp.float32) + dot(h, wdown)).astype(bf))
    return outs


def passed_along(block, axis, distance):
    devices = range(lax.axis_size(axis))
    route = [((i - distance) % len(devices), i) for i in devices]
    return lax.ppermute(block, axis, route)


def to_windows(grid):
    levels, lat_rows, lon_cols = grid.shape[:3]
    trailing = grid.shape[3:]
    shaped = grid.reshape(
        (levels // WZ, WZ, lat_rows // WLAT, WLAT, lon_cols // WLON, WLON) + trailing
    )
    axes_order = (2, 0, 4, 1, 3, 5) + tuple(range(6, 6 + len(trailing)))
    return shaped.transpose(axes_order).reshape(
        (lat_rows // WLAT, levels // WZ * (lon_cols // WLON), WZ * WLAT * WLON) + trailing
    )


def from_windows(windows, levels, lat_rows, lon_cols):
    trailing = windows.shape[3:]
    shaped = windows.reshape(
        (lat_rows // WLAT, levels // WZ, lon_cols // WLON, WZ, WLAT, WLON) + trailing
    )
    axes_order = (1, 3, 0, 4, 2, 5) + tuple(range(6, 6 + len(trailing)))
    return shaped.transpose(axes_order).reshape((levels, lat_rows, lon_cols) + trailing)


def window_kernel(heads, lag, pick, x_ref, tab_ref, g1, wk, wqv, wproj, g2, wup, wdown, o_ref):
    xs = [x_ref[0, w].astype(jnp.float32) for w in range(len(pick))]
    tabs = [tab_ref.at[0, p] for p in pick]
    ys = attend_all(xs, tabs, g1[...], wk[...], wqv[...], wproj[...], heads, lag)
    for w, out in enumerate(ffn_all(ys, g2[...], wup[...], wdown[...])):
        o_ref[0, w] = out


def window_blocks(x, tabs, pick, weights, heads, lag=1):
    rows, amount, win, d = x.shape
    last = rows - 1
    full = lambda a: pl.BlockSpec(a.shape, lambda i: (0,) * a.ndim)
    block = pl.BlockSpec((1, amount, win, d), lambda i: (i, 0, 0, 0))
    return pl.pallas_call(
        functools.partial(window_kernel, heads, lag, pick),
        grid=(rows,),
        out_shape=jax.ShapeDtypeStruct(x.shape, x.dtype),
        in_specs=[
            block,
            pl.BlockSpec((1,) + tabs.shape[1:], lambda i: (jnp.where(i == last, 1, 0), 0, 0, 0)),
        ]
        + [full(a) for a in weights],
        out_specs=block,
    )(x, tabs, *weights)


def bias_tables(bias, closed):
    heads, win = bias.shape[:2]
    base = (bias * math.log2(math.e)).transpose(2, 0, 1)
    position = jnp.arange(win, dtype=jnp.int32)
    level = position // (WLAT * WLON)
    half = (position // WLON) % WLAT // (WLAT // 2)
    apart = lambda g: jnp.where(g[:, None] != g[None, :], -1e30, 0.0).astype(jnp.float32)
    by_level, by_row = apart(level), jnp.where(closed, apart(half), 0.0)

    def lanes(t):
        t = jnp.broadcast_to(t, base.shape)
        main = t[:, :, :128].reshape(win, heads * 128)
        tail = t[:, :, 128:].reshape(win, heads * (win - 128))
        return jnp.concatenate([main, tail, jnp.zeros((win, 128 - tail.shape[1]), t.dtype)], axis=1)

    cuts = [jnp.zeros_like(by_level), by_level, by_row, by_level + by_row]
    tables = jnp.stack([lanes(base + c[:, None, :]) for c in cuts])
    return tables.reshape((2, 2) + tables.shape[1:])


def on_device(
    tokens,
    obs_values,
    obs_dest,
    obs_cell,
    obs_count,
    w_obs,
    ln1_gain,
    w_qkv,
    position_bias,
    w_proj,
    ln2_gain,
    w_up,
    w_down,
):
    levels, lat_rows, lon_cols, features = tokens.shape
    lon_count = lax.axis_size("lon")
    lat_count = lax.axis_size("lat")
    devices = lon_count * lat_count
    row_count = obs_values.shape[0]
    capacity = 2 * row_count // devices
    position = jnp.arange(row_count, dtype=jnp.int32)
    is_live = position < obs_count[0]
    matches = (
        (obs_dest[:, None] == jnp.arange(devices, dtype=jnp.int32)[None, :]) & is_live[:, None]
    ).astype(jnp.int32)
    earlier = jnp.cumsum(matches, axis=0) - matches
    slot_ids = jnp.sum(earlier * matches, axis=1)
    targets = jnp.where(is_live, obs_dest * capacity + slot_ids, devices * capacity)
    cell_ids = jnp.zeros((devices * capacity,), jnp.int32).at[targets].set(obs_cell, mode="drop")
    payload = jnp.dot(obs_values, w_obs, preferred_element_type=jnp.float32).astype(jnp.bfloat16)
    buffer = (
        jnp.zeros((devices * capacity, payload.shape[1]), jnp.bfloat16)
        .at[targets]
        .set(payload, mode="drop")
    )
    received, got_cells = (
        lax.all_to_all(buffer, ("lon", "lat"), split_axis=0, concat_axis=0, tiled=True),
        lax.all_to_all(cell_ids, ("lon", "lat"), split_axis=0, concat_axis=0, tiled=True),
    )
    obs_field = (
        jnp.zeros((levels * lat_rows * lon_cols, features), jnp.float32)
        .at[got_cells]
        .add(received.astype(jnp.float32))
    )
    stream = (tokens.astype(jnp.float32) + obs_field.reshape(tokens.shape)).astype(jnp.bfloat16)
    half_lat = WLAT // 2
    half_lon = WLON // 2
    lat_index = lax.axis_index("lat")
    arrived = passed_along(stream[:, :, :half_lon], "lon", -1)
    widened = jnp.concatenate([stream[:, :, half_lon:], arrived], axis=2)
    arrived = passed_along(widened[:, :half_lat], "lat", -1)
    shifted = jnp.concatenate([widened[:, half_lat:], arrived], axis=1)
    heads = position_bias.shape[0]
    windows = to_windows(jnp.roll(shifted, -(WZ // 2), axis=0))
    tables = bias_tables(position_bias, lat_index == lat_count - 1)
    pairs, across = levels // WZ, lon_cols // WLON
    pick = [1 if p == pairs - 1 else 0 for p in range(pairs) for _ in range(across)]
    w_key = w_qkv[:, features : 2 * features]
    w_rest = jnp.concatenate([w_qkv[:, :features], w_qkv[:, 2 * features :]], axis=1).T
    weights = (ln1_gain[None], w_key, w_rest, w_proj, ln2_gain[None], w_up, w_down)
    done = window_blocks(windows, tables, pick, weights, heads)
    result = jnp.roll(from_windows(done, levels, lat_rows, lon_cols), WZ // 2, axis=0)
    arrived = passed_along(result[:, lat_rows - half_lat :], "lat", 1)
    widened = jnp.concatenate([arrived, result[:, : lat_rows - half_lat]], axis=1)
    arrived = passed_along(widened[:, :, lon_cols - half_lon :], "lon", 1)
    return jnp.concatenate([arrived, widened[:, :, : lon_cols - half_lon]], axis=2)


def solution(mesh):
    in_specs = (
        P(None, "lat", "lon", None),
        P(("lon", "lat"), None),
        P(("lon", "lat")),
        P(("lon", "lat")),
        P(("lon", "lat")),
        P(),
        P(),
        P(),
        P(),
        P(),
        P(),
        P(),
        P(),
    )
    out_specs = P(None, "lat", "lon", None)
    return jax.shard_map(
        on_device, mesh=mesh, in_specs=in_specs, out_specs=out_specs, check_vma=False
    )
```

profile of v0, /device:TPU:0, one launch (start us, length us, event | category | flops | bytes accessed | tf_op | source)
XLA Modules:
  0.0 312.6 jit_solution(15574381634076809715)
XLA Ops:
  1.5 9.1 %reduce-window.6 = s32[32,16,128]{2,1,0:T(8,128)S(1)} reduce-window(s32[32,16,128]{2,1,0:T(8,128)S(1)} %fusion.13, s32[]{:T(128)} %constant.27.clone.1), window={size=1x1x128 pad=0_0x0_0x127_0}, to_apply=%region_0.0 | reduce-window | flops 8323072 | bytes 524292 | tf_op jit(solution)/shard_map/reduce-window
  12.8 8.8 %scatter_custom_fusion = s32[4096]{0:T(1024)} fusion(s32[2048]{0:T(1024)S(1)} %compare_select_fusion.2, s32[2048]{0:T(1024)} %param.16, s32[]{:T(128)} %constant.27.clone.1), kind=kCustom, calls=%fused_computation.50 | custom fusion | bytes 16896 | tf_op jit(solution)/shard_map/scatter | solution.py:208
  21.6 7.3 %all-to-all-start = ((s32[32,128,1]{1,2,0:T(1,128)}), s32[32,128,1]{1,2,0:T(1,128)S(1)}, u32[]{:S(2)}, u32[]{:S(2)}) async-start(s32[32,128,1]{1,2,0:T(1,128)} %bitcast.6), calls=%async_computation | async-start | bytes 32768 | tf_op jit(solution)/shard_map/all_to_all | solution.py:217
  30.9 10.0 %scatter_custom_fusion.1 = bf16[4096,192]{1,0:T(8,128)(2,1)S(1)} fusion(s32[2048]{0:T(1024)S(1)} %compare_select_fusion.2, bf16[2048,192]{1,0:T(8,128)(2,1)S(1)} %copy.91, bf16[]{:T(256)} %constant.53.clone.1), kind=kCustom, calls=%fused_computation.20 | custom fusion | bytes 1572866 | tf_op jit(solution)/shard_map/scatter | solution.py:213
  40.9 2.7 copy.92
  43.6 5.8 %all-to-all-start.1 = ((bf16[32,128,192]{1,2,0:T(8,128)(2,1)}), bf16[32,128,192]{1,2,0:T(8,128)(2,1)S(1)}, u32[]{:S(2)}, u32[]{:S(2)}) async-start(bf16[32,128,192]{1,2,0:T(8,128)(2,1)} %copy.92), calls=%async_computation.1 | async-start | bytes 3145728 | tf_op jit(solution)/shard_map/all_to_all | solution.py:216
  50.9 34.4 %all-to-all-done.1 = bf16[32,128,192]{1,2,0:T(8,128)(2,1)S(1)} async-done(((bf16[32,128,192]{1,2,0:T(8,128)(2,1)}), bf16[32,128,192]{1,2,0:T(8,128)(2,1)S(1)}, u32[]{:S(2)}, u32[]{:S(2)}) %all-to-all-start.1) | async-done | bytes 1572896 | tf_op jit(solution)/shard_map/all_to_all | solution.py:216
  85.3 3.0 copy.113
  88.3 30.8 %scatter_custom_fusion.2 = f32[10368,192]{1,0:T(8,128)} fusion(s32[4096]{0:T(1024)S(1)} %bitcast.91, f32[4096,192]{1,0:T(8,128)} %bitcast.78, f32[]{:T(128)} %constant.26.clone.1), kind=kCustom, calls=%fused_computation.13 | custom fusion | flops 786432 | bytes 7963136 | tf_op jit(solution)/shard_map/scatter-add | solution.py:222
  119.1 9.2 %add_convert_fusion = bf16[6,72,24,192]{3,2,1,0:T(8,128)(2,1)} fusion(f32[6,72,24,192]{3,2,1,0:T(8,128)} %bitcast.71, bf16[6,72,24,192]{3,2,1,0:T(8,128)(2,1)} %param.13), kind=kLoop, calls=%fused_computation.3 | loop fusion | flops 5971968 | bytes 15925248 | tf_op jit(solution)/shard_map/convert_element_type | solution.py:224
  128.3 1.7 slice.107
  131.3 2.8 collective-permute-start
  140.5 1.6 copy.105
  143.1 1.8 fusion.19
  146.9 1.6 maximum_bitcast_fusion
  149.9 3.1 slice.106
  153.0 1.7 copy.96
  155.7 2.1 fusion.4
  157.8 4.0 %collective-permute-done.1 = bf16[6,3,24,192]{3,2,1,0:T(8,128)(2,1)S(1)} collective-permute-done((bf16[6,3,24,192]{3,2,1,0:T(8,128)(2,1)S(1)}, bf16[6,3,24,192]{3,2,1,0:T(8,128)(2,1)S(1)}, u32[]{:S(2)}, u32[]{:S(2)}) %collective-permute-start.1) | collective-permute-done | bytes 165920 | tf_op jit(solution)/shard_map/ppermute | solution.py:109
  163.0 3.0 fusion.1
  166.0 10.2 %reshape.274 = bf16[3,2,12,6,2,12,192]{6,5,4,3,2,1,0:T(8,128)(2,1)} reshape(bf16[6,72,24,192]{3,2,1,0:T(8,128)(2,1)} %fusion.1) | data formatting | bytes 7962624 | tf_op jit(solution)/shard_map/reshape | solution.py:115
  176.2 7.0 %copy.97 = bf16[12,3,2,2,6,12,192]{6,5,4,3,2,1,0:T(8,128)(2,1)} copy(bf16[12,3,2,2,6,12,192]{6,5,2,4,0,3,1:T(8,128)(2,1)} %bitcast.74) | data formatting | bytes 7962624 | tf_op jit(solution)/shard_map/transpose | solution.py:119
  183.2 10.3 %reshape.275.x_ref = bf16[12,6,144,192]{3,2,1,0:T(8,128)(2,1)} reshape(bf16[12,3,2,2,6,12,192]{6,5,4,3,2,1,0:T(8,128)(2,1)} %copy.97) | data formatting | bytes 7962624 | tf_op jit(solution)/shard_map/reshape | solution.py:119
  193.5 54.9 %shard_map.127 = bf16[12,6,144,192]{3,2,1,0:T(8,128)(2,1)} custom-call(bf16[12,6,144,192]{3,2,1,0:T(8,128)(2,1)} %reshape.275.x_ref, f32[2,2,144,896]{3,2,1,0:T(8,128)} %bitcast.77, f32[1,192]{1,0:T(1,128)} %bitcast.92, bf16[192,192]{1,0:T(8,128)(2,1)} %get-tuple-element.9.wk, bf16[384,192]{1,0:T(8,128)(2,1)} %maximum_bitcast_fusion.4.wqv, ...), custom_call_target="tpu_custom_call" | custom-call | tf_op jit(solution)/shard_map/pallas_call | solution.py:146
  248.4 10.2 %reshape.285 = bf16[12,3,2,2,6,12,192]{6,5,4,3,2,1,0:T(8,128)(2,1)} reshape(bf16[12,6,144,192]{3,2,1,0:T(8,128)(2,1)} %shard_map.127) | data formatting | bytes 7962624 | tf_op jit(solution)/shard_map/reshape | solution.py:126
  258.6 7.0 %copy.109 = bf16[3,2,12,6,2,12,192]{6,5,4,3,2,1,0:T(8,128)(2,1)} copy(bf16[3,2,12,6,2,12,192]{6,5,3,1,4,0,2:T(8,128)(2,1)} %bitcast.75) | data formatting | bytes 7962624 | tf_op jit(solution)/shard_map/transpose | solution.py:130
  265.6 10.3 %reshape.286 = bf16[6,72,24,192]{3,2,1,0:T(8,128)(2,1)} reshape(bf16[3,2,12,6,2,12,192]{6,5,4,3,2,1,0:T(8,128)(2,1)} %copy.109) | data formatting | bytes 7962624 | tf_op jit(solution)/shard_map/reshape | solution.py:130
  275.9 2.5 slice.121
  279.7 1.8 collective-permute-start.2
  281.5 7.1 %collective-permute-done.2 = bf16[6,3,24,192]{3,2,1,0:T(8,128)(2,1)S(1)} collective-permute-done((bf16[6,3,24,192]{3,2,1,0:T(8,128)(2,1)S(1)}, bf16[6,3,24,192]{3,2,1,0:T(8,128)(2,1)S(1)}, u32[]{:S(2)}, u32[]{:S(2)}) %collective-permute-start.2) | collective-permute-done | bytes 165920 | tf_op jit(solution)/shard_map/ppermute | solution.py:109
  289.4 18.1 %collective-permute-done.3 = bf16[6,72,6,192]{3,1,2,0:T(8,128)(2,1)S(1)} collective-permute-done((bf16[6,72,6,192]{3,1,2,0:T(8,128)(2,1)S(1)}, bf16[6,72,6,192]{3,1,2,0:T(8,128)(2,1)S(1)}, u32[]{:S(2)}, u32[]{:S(2)}) %collective-permute-start.3) | collective-permute-done | bytes 995360 | tf_op jit(solution)/shard_map/ppermute | solution.py:109
  307.9 4.7 %fusion = bf16[6,72,24,192]{3,2,1,0:T(8,128)(2,1)} fusion(bf16[6,3,24,192]{3,2,1,0:T(8,128)(2,1)S(1)} %collective-permute-done.2, bf16[5,72,24,192]{3,2,1,0:T(8,128)(2,1)S(1)} %slice.121, bf16[1,72,24,192]{3,2,1,0:T(8,128)(2,1)S(1)} %slice.120, bf16[6,72,6,192]{3,2,1,0:T(8,128)(2,1)S(1)} %copy.111), kind=kLoop, calls=%fused_computation.5 | loop fusion | flops 15925248 | bytes 9123840 | tf_op jit(solution)/shard_map/concatenate | solution.py:245
  (71 shorter events, 23.1 us)
Async XLA Ops:
  0.0 28.9 %copy-start = (bf16[2048,256]{1,0:T(8,128)(2,1)S(1)}, bf16[2048,256]{1,0:T(8,128)(2,1)}, u32[]{:S(2)}) copy-start(bf16[2048,256]{1,0:T(8,128)(2,1)} %param.14) | copy-start | bytes 3145732
  21.6 22.0 %all-to-all-start = ((s32[32,128,1]{1,2,0:T(1,128)}), s32[32,128,1]{1,2,0:T(1,128)S(1)}, u32[]{:S(2)}, u32[]{:S(2)}) async-start(s32[32,128,1]{1,2,0:T(1,128)} %bitcast.6), calls=%async_computation | async-start | bytes 32768 | tf_op jit(solution)/shard_map/all_to_all | solution.py:217
  43.6 41.7 %all-to-all-start.1 = ((bf16[32,128,192]{1,2,0:T(8,128)(2,1)}), bf16[32,128,192]{1,2,0:T(8,128)(2,1)S(1)}, u32[]{:S(2)}, u32[]{:S(2)}) async-start(bf16[32,128,192]{1,2,0:T(8,128)(2,1)} %copy.92), calls=%async_computation.1 | async-start | bytes 3145728 | tf_op jit(solution)/shard_map/all_to_all | solution.py:216
  50.7 68.4 %copy-start.2 = (f32[144,6,144]{0,2,1:T(8,128)}, f32[144,6,144]{0,2,1:T(8,128)S(1)}, u32[]{:S(2)}) copy-start(f32[144,6,144]{0,2,1:T(8,128)S(1)} %multiply_bitcast_fusion) | copy-start | bytes 1492996
  128.3 5.8 %copy-start.3 = (f32[6,144,144]{2,1,0:T(8,128)S(1)}, f32[6,144,144]{2,1,0:T(8,128)}, u32[]{:S(2)}) copy-start(f32[6,144,144]{2,1,0:T(8,128)} %param.21) | copy-start | bytes 1492996
  131.3 3.9 %slice-start.2 = ((f32[144,6,144]{0,2,1:T(8,128)}), f32[144,6,16]{0,2,1:T(8,128)S(1)}, s32[]{:S(2)}) async-start(f32[144,6,144]{0,2,1:T(8,128)} %copy-done.2), calls=%async_computation.4 | async-start | bytes 196608 | tf_op jit(solution)/shard_map/slice | solution.py:171
  131.3 4.7 %slice-start.3 = ((f32[144,6,144]{0,2,1:T(8,128)}), f32[144,6,128]{0,2,1:T(8,128)S(1)}, s32[]{:S(2)}) async-start(f32[144,6,144]{0,2,1:T(8,128)} %copy-done.2), calls=%async_computation.5 | async-start | bytes 1572864 | tf_op jit(solution)/shard_map/slice | solution.py:170
  131.3 21.7 %collective-permute-start = (bf16[6,72,6,192]{3,1,2,0:T(8,128)(2,1)}, bf16[6,72,6,192]{3,1,2,0:T(8,128)(2,1)}, u32[]{:S(2)}, u32[]{:S(2)}) collective-permute-start(bf16[6,72,6,192]{3,1,2,0:T(8,128)(2,1)} %copy.95), channel_id=1, source_target_pairs={{4,0},{8,4},{12,8},{16,12},{20,16},{24,20},{28,24},{0,28},{5,1},{9... | collective-permute-start | bytes 2985992 | tf_op jit(solution)/shard_map/ppermute | solution.py:109
  137.0 8.2 %copy-start.6 = (bf16[768,192]{0,1:T(8,128)(2,1)S(1)}, bf16[768,192]{0,1:T(8,128)(2,1)}, u32[]{:S(2)}) copy-start(bf16[768,192]{0,1:T(8,128)(2,1)} %param.25) | copy-start | bytes 884740
  138.7 8.2 %copy-start.4 = (f32[144,768]{1,0:T(8,128)S(1)}, f32[144,768]{1,0:T(8,128)}, u32[]{:S(2)}) copy-start(f32[144,768]{1,0:T(8,128)} %copy.98) | copy-start | bytes 1327108
  138.7 8.2 %copy-start.5 = (f32[144,768]{1,0:T(8,128)S(1)}, f32[144,768]{1,0:T(8,128)}, u32[]{:S(2)}) copy-start(f32[144,768]{1,0:T(8,128)} %copy.100) | copy-start | bytes 1327108
  143.1 6.8 %slice-start = ((s8[5308416]{0:T(1024)(128)(4,1)}), s8[1114112]{0:T(1024)(128)(4,1)S(1)}, s32[]{:S(2)}) async-start(s8[5308416]{0:T(1024)(128)(4,1)} %bitcast.72), calls=%async_computation.2 | async-start | bytes 2228224
  146.9 3.0 slice-start.1
  154.7 7.1 %collective-permute-start.1 = (bf16[6,3,24,192]{3,2,1,0:T(8,128)(2,1)S(1)}, bf16[6,3,24,192]{3,2,1,0:T(8,128)(2,1)S(1)}, u32[]{:S(2)}, u32[]{:S(2)}) collective-permute-start(bf16[6,3,24,192]{3,2,1,0:T(8,128)(2,1)S(1)} %pad_maximum_fusion.6), channel_id=1, source_target_pairs={{1,0},{2,1},{3,2},{0,3},{5,4},{6,5},{7,6},{4,7},{9,8},{10,9},{11,1... | collective-permute-start | bytes 497672 | tf_op jit(solution)/shard_map/ppermute | solution.py:109
  279.7 8.9 %collective-permute-start.2 = (bf16[6,3,24,192]{3,2,1,0:T(8,128)(2,1)S(1)}, bf16[6,3,24,192]{3,2,1,0:T(8,128)(2,1)S(1)}, u32[]{:S(2)}, u32[]{:S(2)}) collective-permute-start(bf16[6,3,24,192]{3,2,1,0:T(8,128)(2,1)S(1)} %pad_maximum_fusion.5), channel_id=1, source_target_pairs={{3,0},{0,1},{1,2},{2,3},{7,4},{4,5},{5,6},{6,7},{11,8},{8,9},{9,10... | collective-permute-start | bytes 497672 | tf_op jit(solution)/shard_map/ppermute | solution.py:109
  289.3 18.2 %collective-permute-start.3 = (bf16[6,72,6,192]{3,1,2,0:T(8,128)(2,1)S(1)}, bf16[6,72,6,192]{3,1,2,0:T(8,128)(2,1)S(1)}, u32[]{:S(2)}, u32[]{:S(2)}) collective-permute-start(bf16[6,72,6,192]{3,1,2,0:T(8,128)(2,1)S(1)} %copy.110), channel_id=1, source_target_pairs={{28,0},{0,4},{4,8},{8,12},{12,16},{16,20},{20,24},{24,28},{29,1},{... | collective-permute-start | bytes 2985992 | tf_op jit(solution)/shard_map/ppermute | solution.py:109
  307.5 5.1 %copy-start.1 = (bf16[2048,256]{1,0:T(8,128)(2,1)S(1)}, bf16[2048,256]{1,0:T(8,128)(2,1)}, u32[]{:S(2)}) copy-start(bf16[2048,256]{1,0:T(8,128)(2,1)} %param.14) | copy-start | bytes 3145732
where the time goes:
time: 314 us; the launch traced here: 313 us
  local copies, waits for them, and re-layouts  104 us (33%)
  other arithmetic  68.7 us (22%)
  waiting for transfers between devices  63.5 us (20%)
  Pallas kernels  54.9 us (17%)
  starting transfers between devices  18.8 us (6%)
    pallas_call x1, Pallas kernels, window_blocks(): pl.pallas_call(functools.partial(window_kernel, heads, lag, pick), grid=(...  54.9 us
    all_to_all x1, waiting for transfers between devices, on_device(): lax.all_to_all(buffer, ('lon', 'lat'), split_axis=0, concat_axis=0, tiled...  34.4 us
    scatter-add x1, other arithmetic, on_device(): obs_field = jnp.zeros((levels * lat_rows * lon_cols, features), jnp.float...  30.8 us
    ppermute x4, waiting for transfers between devices, passed_along(): return lax.ppermute(block, axis, route)  29.1 us
    reshape x1, local copies, waits for them, and re-layouts, to_windows(): shaped.transpose(axes_order)  10.3 us
    reshape x1, local copies, waits for them, and re-layouts, from_windows(): shaped.transpose(axes_order)  10.3 us
    reshape x1, local copies, waits for them, and re-layouts, to_windows(): grid.reshape((levels // WZ, WZ, lat_rows // WLAT, WLAT, lon_cols // WLON,...  10.2 us
    reshape x1, local copies, waits for them, and re-layouts, from_windows(): windows.reshape((lat_rows // WLAT, levels // WZ, lon_cols // WLON, WZ, WL...  10.2 us
  transfers between devices with their start and end apart: 6, of which 4 were waited for; matrix products, arithmetic and copies ran while one was open for 12% of the time, Pallas kernels for 0%

commit v1 on v0

v1 whole, which is shorter than its diff:
```python
import functools
import math

import jax
import jax.numpy as jnp
import numpy as np
from jax import lax
from jax.experimental import pallas as pl
from jax.experimental.pallas import tpu as pltpu
from jax.sharding import PartitionSpec as P

WZ = 2
WLAT = 6
WLON = 12

NT = (((1,), (1,)), ((), ()))
TN = (((0,), (0,)), ((), ()))


def layer_norm(x, gain):
    n = x.shape[-1]
    mean = jnp.sum(x, axis=-1, keepdims=True) * (1.0 / n)
    c = x - mean
    var = jnp.sum(c * c, axis=-1, keepdims=True) * (1.0 / n)
    return c * lax.rsqrt(var + 1e-5) * gain


def dot(a, b):
    return jnp.dot(a, b, preferred_element_type=jnp.float32)


def attend_all(xs, tabs, g1, wk, wqv, wproj, heads, lag=1):
    bf, f32 = jnp.bfloat16, jnp.float32
    win, d = xs[0].shape
    hd, tail = d // heads, win - 128
    reps, n = 128 // tail, len(xs)
    nx = [layer_norm(x, g1).astype(bf) for x in xs]
    kk, q, v = [], [], []
    for i in range(n):
        kk.append(dot(nx[i], wk).astype(bf))
        ext = jnp.concatenate([nx[i][:128]] + [nx[i][128:]] * reps, axis=0)
        qv = lax.dot_general(wqv, ext, NT, preferred_element_type=f32)
        q.append((qv[:d] * (math.log2(math.e) / math.sqrt(hd))).astype(bf))
        v.append(qv[d:].astype(bf)[:, :win])
    ones = jnp.ones((16, win), bf)
    zero = jnp.zeros((hd, 128), bf)
    mask = (lax.broadcasted_iota(jnp.int32, (d, 128), 0) // hd) == (lax.broadcasted_iota(jnp.int32, (d, 128), 1) // tail)
    jobs = [(i, p) for i in range(n) for p in range(heads // 2 + 1)]
    s_of, e_of, c_of = {}, {}, {}

    def scores(i, p):
        if p < heads // 2:
            cols = [jnp.concatenate([q[i][hd * h:hd * h + hd, :128] if j == h else zero for j in range(heads)], axis=0)
                    for h in (2 * p, 2 * p + 1)]
            rhs = jnp.concatenate(cols, axis=1)
        else:
            rhs = jnp.where(mask, q[i][:, 128:].astype(f32), 0.0).astype(bf)
        s_of[i, p] = dot(kk[i], rhs) + tabs[i][:, 256 * p:256 * p + rhs.shape[1]]

    def soft(i, p):
        s = s_of.pop((i, p))
        e_of[i, p] = jnp.exp2(s - jnp.max(s, axis=0, keepdims=True)).astype(bf)

    def values(i, p):
        e = e_of.pop((i, p))
        if p < heads // 2:
            o = dot(jnp.concatenate([v[i][2 * hd * p:2 * hd * p + 2 * hd], ones], axis=0), e)
            r = 1.0 / o[2 * hd:2 * hd + 1]
            c_of[i, p] = [(o[:hd, :128] * r[:, :128]).astype(bf), (o[hd:2 * hd, 128:] * r[:, 128:]).astype(bf)]
        else:
            o = dot(jnp.concatenate([v[i], ones], axis=0), e)
            c_of[i, p] = jnp.where(mask, o[:d] * (1.0 / o[d:d + 1]), 0.0).astype(bf)

    ys = []
    def finish(i):
        main = jnp.concatenate([c for p in range(heads // 2) for c in c_of[i, p]], axis=0)
        ctx = jnp.concatenate([main, c_of[i, heads // 2]], axis=1)
        proj = lax.dot_general(ctx, wproj, TN, preferred_element_type=f32)
        fold = proj[128:128 + tail]
        for h in range(1, heads):
            fold = fold + proj[128 + tail * h:128 + tail * h + tail]
        ys.append((xs[i] + jnp.concatenate([proj[:128], fold], axis=0)).astype(bf))

    for t in range(len(jobs) + 2 * lag):
        if t < len(jobs):
            scores(*jobs[t])
        if 0 <= t - lag < len(jobs):
            soft(*jobs[t - lag])
        if 0 <= t - 2 * lag < len(jobs):
            values(*jobs[t - 2 * lag])
            if jobs[t - 2 * lag][1] == heads // 2:
                finish(jobs[t - 2 * lag][0])
    return ys


def ffn_all(ys, g2, wup, wdown):
    bf = jnp.bfloat16
    n2 = [layer_norm(y.astype(jnp.float32), g2).astype(bf) for y in ys]
    outs = []
    for i in range(len(ys)):
        u = dot(n2[i], wup)
        h = (0.5 * u * (1.0 + lax.erf(u * (1.0 / math.sqrt(2.0))))).astype(bf)
        outs.append((ys[i].astype(jnp.float32) + dot(h, wdown)).astype(bf))
    return outs


def window_kernel(heads, amount, *refs):
    tab_ref, last_ref, g1, wk, wqv, wproj, g2, wup, wdown = refs[amount : amount + 9]
    outs = refs[-amount:]
    rows, pairs = refs[0].shape[:2]
    xs, tabs = [], []
    for r in range(rows):
        for p in range(pairs):
            parts = [x[r, p].astype(jnp.float32) for x in refs[:amount]]
            xs.append(parts[0] if amount == 1 else jnp.concatenate(parts, axis=0))
            cut = 1 if p == pairs - 1 else 0
            tabs.append(last_ref.at[0, cut] if r == rows - 1 else tab_ref.at[0, cut])
    ys = attend_all(xs, tabs, g1[...], wk[...], wqv[...], wproj[...], heads)
    for w, y in enumerate(ffn_all(ys, g2[...], wup[...], wdown[...])):
        first = 0
        for o in outs:
            size = o.shape[2]
            piece = y if amount == 1 else y.astype(jnp.float32)[first : first + size].astype(y.dtype)
            o[w // pairs, w % pairs] = piece
            first += size


def window_blocks(arrays, tables, weights, heads, steps, in_step, out_step, total, wraps, kept=None):
    pairs = arrays[0].shape[1]
    full = lambda a: pl.BlockSpec(a.shape, lambda i: (0,) * a.ndim)
    rows = lambda a, first: pl.BlockSpec((2,) + a.shape[1:], lambda i: (first + i, 0, 0, 0))
    table = lambda pick: pl.BlockSpec((1,) + tables.shape[1:], pick)
    last = lambda i: (jnp.where(i == steps - 1, 1, 0) if wraps else 0, 0, 0, 0)
    shapes = [jax.ShapeDtypeStruct((total,) + a.shape[1:], a.dtype) for a in arrays]
    specs = [rows(a, in_step) for a in arrays] + [table(lambda i: (0, 0, 0, 0)), table(last)]
    specs = specs + [full(a) for a in weights]
    operands = list(arrays) + [tables, tables] + list(weights)
    aliases = {}
    if kept is not None:
        specs.append(pl.BlockSpec(memory_space=pl.ANY))
        aliases = {len(operands): 0}
        operands.append(kept)
    tokens = steps * 2 * pairs * sum(a.shape[2] for a in arrays)
    return pl.pallas_call(
        functools.partial(window_kernel, heads, len(arrays)),
        grid=(steps,),
        out_shape=shapes,
        in_specs=specs,
        out_specs=[rows(a, out_step) for a in arrays],
        input_output_aliases=aliases,
        cost_estimate=pl.CostEstimate(flops=tokens * 2000000, bytes_accessed=tokens * 800, transcendentals=tokens * 1500),
    )(*operands)


def bias_tables(bias, closed, order):
    heads, win = bias.shape[:2]
    base = (bias[:, order][:, :, order] * math.log2(math.e)).transpose(2, 0, 1)
    level = order // (WLAT * WLON)
    half = (order // WLON) % WLAT // (WLAT // 2)
    apart = lambda g: np.where(g[:, None] != g[None, :], -1e30, 0.0).astype(np.float32)
    by_level, by_row = apart(level), jnp.where(closed, apart(half), 0.0)

    def lanes(t):
        main = t[:, :, :128].reshape(win, heads * 128)
        tail = t[:, :, 128:].reshape(win, heads * (win - 128))
        return jnp.concatenate([main, tail, jnp.zeros((win, 128 - tail.shape[1]), t.dtype)], axis=1)

    plain = lanes(base)
    spread = lambda c: lanes(jnp.broadcast_to(c[:, None, :], base.shape))
    cuts = [jnp.zeros_like(plain), spread(by_level), spread(by_row), spread(by_level + by_row)]
    tables = jnp.stack([plain + c for c in cuts])
    return tables.reshape((2, 2) + tables.shape[1:])


def token_order(first_col, cols):
    half, level, row, col = np.meshgrid(
        np.arange(2), np.arange(WZ), np.arange(WLAT // 2), np.arange(cols), indexing="ij"
    )
    return ((level * WLAT + half * (WLAT // 2) + row) * WLON + first_col + col).reshape(-1)


def dispatch_kernel(cap, total, count_ref, dest_ref, payload_ref, out_ref, target_ref):
    bf, f32, i32 = jnp.bfloat16, jnp.float32, jnp.int32
    n = dest_ref.shape[1]
    group = out_ref.shape[0]

    @pl.when(pl.program_id(0) == 0)
    def _():
        dest = dest_ref[...]
        lane = lax.broadcasted_iota(i32, (1, n), 1)
        owner = lax.broadcasted_iota(i32, (total, n), 0)
        hit = (dest == owner) & (lane < count_ref[0])
        hits = jnp.where(hit, 1.0, 0.0)
        upper = lax.broadcasted_iota(i32, (128, 128), 0) < lax.broadcasted_iota(i32, (128, 128), 1)
        upper = jnp.where(upper, 1.0, 0.0).astype(bf)
        base = (lax.broadcasted_iota(i32, (total, 1), 0) * cap).astype(f32)
        for b in range(n // 128):
            block = hits[:, 128 * b : 128 * b + 128]
            slot = dot(block.astype(bf), upper) + base
            found = jnp.sum(block * slot, axis=0, keepdims=True)
            live = jnp.sum(block, axis=0, keepdims=True)
            target_ref[:, 128 * b : 128 * b + 128] = jnp.where(live > 0.5, found, -1.0).astype(i32)
            base = base + jnp.sum(block, axis=1, keepdims=True)

    rows = group * cap
    slot = pl.program_id(0) * rows + lax.broadcasted_iota(i32, (rows, 1), 0)
    chosen = jnp.where(target_ref[...] == slot, 1.0, 0.0).astype(bf)
    moved = dot(chosen, payload_ref[...])
    pick = lax.broadcasted_iota(i32, (8, 128), 0) + 64 == lax.broadcasted_iota(i32, (8, 128), 1)
    pick = jnp.where(pick, 1.0, 0.0).astype(bf)
    low = lax.broadcasted_iota(i32, (cap // 2, 128), 1) < 64
    for g in range(group):
        part = moved[g * cap : g * cap + cap]
        tail = part[:, 128:]
        packed = jnp.where(low, tail[: cap // 2], pltpu.roll(tail[cap // 2 :], 64, 1))
        cells = lax.dot_general(pick, tail.astype(bf), NT, preferred_element_type=f32)
        if cap < 128:
            cells = jnp.concatenate([cells, jnp.zeros((8, 128 - cap), f32)], axis=1)
        out_ref[g] = jnp.concatenate([part[:, :128], packed, cells], axis=0).astype(bf)


def dispatch(count, dest, payload, devices, cap):
    group = 512 // cap
    rows = cap + cap // 2 + 8
    n = dest.shape[0]
    return pl.pallas_call(
        functools.partial(dispatch_kernel, cap, devices),
        grid=(devices // group,),
        out_shape=jax.ShapeDtypeStruct((devices, rows, 128), jnp.bfloat16),
        in_specs=[
            pl.BlockSpec(memory_space=pltpu.SMEM),
            pl.BlockSpec((1, n), lambda i: (0, 0)),
            pl.BlockSpec(payload.shape, lambda i: (0, 0)),
        ],
        out_specs=pl.BlockSpec((group, rows, 128), lambda i: (i, 0, 0)),
        scratch_shapes=[pltpu.VMEM((1, n), jnp.int32)],
    )(count, dest[None], payload)


def collect_kernel(cap, levels, lat_rows, codes, got, tok, mid, right, left, field, held, win):
    bf, f32, i32 = jnp.bfloat16, jnp.float32, jnp.int32
    lines, features = tok.shape[0], tok.shape[2]
    rest = features - 128

    def fill(q, _):
        t = tok[q].astype(f32)
        field[0, q] = t[:, :128]
        field[1, q, :, :rest] = t[:, 128:]
        field[1, q, :, rest:] = jnp.zeros((t.shape[0], 128 - rest), f32)
        return 0

    lax.fori_loop(0, lines, fill, 0, unroll=4)
    rowi = lax.broadcasted_iota(i32, (cap, cap), 0)
    coli = lax.broadcasted_iota(i32, (cap, cap), 1)
    ones = jnp.ones((cap, cap), bf)
    near = (rowi // 8 == coli // 8) & (coli <= rowi)

    def source(s, _):
        digits = got[s, cap + cap // 2 :, :].astype(f32)
        same = near
        for k in range(2):
            along = jnp.broadcast_to(digits[k : k + 1, :cap], (cap, cap))
            down = dot(jnp.where(rowi == coli, along, 0.0).astype(bf), ones)
            same = same & (along == down)
        same = jnp.where(same, 1.0, 0.0).astype(bf)
        held[0] = dot(same, got[s, :cap, :])
        t = got[s, cap : cap + cap // 2, :].astype(f32)
        held[1] = dot(same, jnp.concatenate([t, pltpu.roll(t, 64, 1)], axis=0).astype(bf))

        for b in range(cap // 8):
            places = [codes[s * cap + 8 * b + j] for j in range(8)]
            spots = [(c >> 5, pl.ds(c & 31, 1)) for c in places]
            sums = [[field[k, q, o, :] + held[k, 8 * b + j : 8 * b + j + 1, :] for k in range(2)]
                    for j, (q, o) in enumerate(spots)]
            for (q, o), pair in zip(spots, sums):
                for k in range(2):
                    field[k, q, o, :] = pair[k]
        return 0

    lax.fori_loop(0, got.shape[0], source, 0)
    half_lat, pairs = WLAT // 2, levels // WZ
    wins = lat_rows // WLAT

    def cut(l, _):
        for p in range(pairs):
            for out, first, cols in ((mid, WLON // 2, WLON), (right, WLON + WLON // 2, WLON // 2), (left, 0, WLON // 2)):
                at = 0
                for half in range(2):
                    for lev in range(WZ):
                        z = (WZ * p + WZ // 2 + lev) % levels
                        for row in range(half_lat):
                            a = half_lat + WLAT * l + half_lat * half + row
                            a = jnp.where(a >= lat_rows, a - lat_rows, a)
                            for k in range(2):
                                win[k, at : at + cols, :] = field[k, z * lat_rows + a, first : first + cols, :]
                            at += cols
                out[l, p, :, :128] = win[0, :at, :].astype(bf)
                out[l, p, :, 128:] = win[1, :at, :rest].astype(bf)
        return 0

    lax.fori_loop(0, wins, cut, 0)


def collect(codes, got, tokens, cap):
    levels, lat_rows, lon_cols, features = tokens.shape
    wins, pairs = lat_rows // WLAT, levels // WZ
    shape = lambda t: jax.ShapeDtypeStruct((wins, pairs, t, features), jnp.bfloat16)
    full, part = WZ * WLAT * WLON, WZ * WLAT * WLON // 2
    lines = levels * lat_rows
    vmem = pl.BlockSpec(memory_space=pltpu.VMEM)
    return pl.pallas_call(
        functools.partial(collect_kernel, cap, levels, lat_rows),
        out_shape=[shape(full), shape(part), shape(part)],
        in_specs=[pl.BlockSpec(memory_space=pltpu.SMEM), vmem, vmem],
        out_specs=[vmem] * 3,
        scratch_shapes=[
            pltpu.VMEM((2, lines, lon_cols, 128), jnp.float32),
            pltpu.VMEM((2, cap, 128), jnp.float32),
            pltpu.VMEM((2, full, 128), jnp.float32),
        ],
    )(codes, got, tokens.reshape(lines, lon_cols, features))


def join_kernel(levels, mid, right, left, out, win):
    f32 = jnp.float32
    half_lat, pairs = WLAT // 2, levels // WZ
    rest = out.shape[3] - 128
    half = (pl.program_id(0) + 2 * pl.num_programs(0) - 1) % 2
    for p in range(pairs):
        base = 0
        for part, cols in ((left, WLON // 2), (mid, WLON), (right, WLON // 2)):
            x = part[0, p].astype(f32)
            if part is mid:
                size = x.shape[0]
            else:
                size = x.shape[0] // 2
                x = jnp.where(half == 0, x[:size], x[size:])
            at = 0
            for lev in range(WZ):
                z = (WZ * p + WZ // 2 + lev) % levels
                for row in range(half_lat):
                    piece = x[at : at + cols]
                    win[0, z * half_lat + row, base : base + cols, :] = piece[:, :128]
                    win[1, z * half_lat + row, base : base + cols, :rest] = piece[:, 128:]
                    at += cols
            base += cols
    for z in range(levels):
        for row in range(half_lat):
            out[z, row, :, :128] = win[0, z * half_lat + row].astype(out.dtype)
            out[z, row, :, 128:] = win[1, z * half_lat + row, :, :rest].astype(out.dtype)


def join(mid, right, left, levels, lat_rows, lon_cols):
    half_lat = WLAT // 2
    units = lat_rows // half_lat
    features = mid.shape[-1]
    unit = lambda u: (u + units - 1) % units
    whole = lambda a: pl.BlockSpec((1,) + a.shape[1:], lambda u: (unit(u) // 2, 0, 0, 0))
    halved = pl.BlockSpec((1, mid.shape[1], mid.shape[2] // 2, features), lambda u: (unit(u) // 2, 0, unit(u) % 2, 0))
    return pl.pallas_call(
        functools.partial(join_kernel, levels),
        grid=(units,),
        out_shape=jax.ShapeDtypeStruct((levels, lat_rows, lon_cols, features), mid.dtype),
        in_specs=[halved, whole(right), whole(left)],
        out_specs=pl.BlockSpec((levels, half_lat, lon_cols, features), lambda u: (0, u, 0, 0)),
        scratch_shapes=[pltpu.VMEM((2, levels * half_lat, lon_cols, 128), jnp.float32)],
    )(mid, right, left)


def sent(block, lon, lat):
    lons, lats = lax.axis_size("lon"), lax.axis_size("lat")
    at = lambda i, j: (i % lons) * lats + j % lats
    route = [(at(i, j), at(i + lon, j + lat)) for i in range(lons) for j in range(lats)]
    return lax.ppermute(block, ("lon", "lat"), route)


def on_device(
    tokens,
    obs_values,
    obs_dest,
    obs_cell,
    obs_count,
    w_obs,
    ln1_gain,
    w_qkv,
    position_bias,
    w_proj,
    ln2_gain,
    w_up,
    w_down,
):
    levels, lat_rows, lon_cols, features = tokens.shape
    lat_count = lax.axis_size("lat")
    devices = lax.axis_size("lon") * lat_count
    row_count = obs_values.shape[0]
    cap = 2 * row_count // devices
    bf = jnp.bfloat16
    payload = jnp.dot(obs_values, w_obs, preferred_element_type=jnp.float32).astype(bf)
    digits = jnp.stack([obs_cell // 128, obs_cell % 128], axis=1).astype(bf)
    payload = jnp.concatenate([payload, digits, jnp.zeros((row_count, 62), bf)], axis=1)
    buffer = dispatch(obs_count, obs_dest, payload, devices, cap)
    got = lax.all_to_all(buffer, ("lon", "lat"), split_axis=0, concat_axis=0, tiled=True)
    body = cap + cap // 2
    high, low = (got[:, body + k, :cap].astype(jnp.int32) for k in range(2))
    cells = (high * 128 + low).reshape(-1)
    codes = (cells // lon_cols) * 32 + cells % lon_cols

    heads = position_bias.shape[0]
    closed = lax.axis_index("lat") == lat_count - 1
    half = WLON // 2
    inner = bias_tables(position_bias, closed, token_order(0, WLON))
    outer = np.concatenate([token_order(0, half), token_order(half, half)])
    outer = bias_tables(position_bias, closed, outer)
    w_key = w_qkv[:, features : 2 * features]
    w_rest = jnp.concatenate([w_qkv[:, :features], w_qkv[:, 2 * features :]], axis=1).T
    weights = (ln1_gain[None], w_key, w_rest, w_proj, ln2_gain[None], w_up, w_down)

    mid, right, left = collect(codes, got, tokens, cap)
    wins = mid.shape[0]
    part = right.shape[2] // 2
    arrived = sent(left, -1, 0)
    below_mid = sent(mid[-1:, :, 2 * part :], 0, -1)
    below_right = sent(right[-1:, :, part:], 0, -1)
    below_left = sent(left[-1:, :, part:], -1, -1)

    first = wins // 2 // 2
    tail = wins // 2 - 1
    done = window_blocks([mid], inner, weights, heads, first, 0, 0, wins, False)[0]
    right_in = lax.dynamic_update_slice(right, below_right, (wins - 1, 0, part, 0))
    left_in = lax.dynamic_update_slice(arrived, below_left, (wins - 1, 0, part, 0))
    right_out, left_out = window_blocks([right_in, left_in], outer, weights, heads, wins // 2, 0, 0, wins, True)
    home_left = sent(left_out, 1, 0)
    home_right = sent(right_out[-1:, :, part:], 0, 1)
    home_corner = sent(left_out[-1:, :, part:], 1, 1)
    edge = jnp.concatenate([mid[-1:, :, : 2 * part], below_mid], axis=2)
    edge = jnp.concatenate([mid[-2:-1], edge], axis=0)
    done = window_blocks([edge], inner, weights, heads, 1, 0, tail, wins, True, done)[0]
    home_mid = sent(done[-1:, :, 2 * part :], 0, 1)
    done = window_blocks([mid], inner, weights, heads, tail - first, first, first, wins, False, done)[0]

    done = lax.dynamic_update_slice(done, home_mid, (wins - 1, 0, 2 * part, 0))
    right_out = lax.dynamic_update_slice(right_out, home_right, (wins - 1, 0, part, 0))
    home_left = lax.dynamic_update_slice(home_left, home_corner, (wins - 1, 0, part, 0))
    return join(done, right_out, home_left, levels, lat_rows, lon_cols)


def solution(mesh):
    in_specs = (
        P(None, "lat", "lon", None),
        P(("lon", "lat"), None),
        P(("lon", "lat")),
        P(("lon", "lat")),
        P(("lon", "lat")),
        P(),
        P(),
        P(),
        P(),
        P(),
        P(),
        P(),
        P(),
    )
    out_specs = P(None, "lat", "lon", None)
    return jax.shard_map(
        on_device, mesh=mesh, in_specs=in_specs, out_specs=out_specs, check_vma=False
    )
```

time: 314 us -> 221 us (0.70)
  Pallas kernels: 54.9 us -> 115 us
  waiting for transfers between devices: 63.5 us -> 4.82 us
  other arithmetic: 68.7 us -> 14.8 us
  local copies, waits for them, and re-layouts: 104 us -> 64 us
    pallas_call x1 -> x7, Pallas kernels: 54.9 us -> 115 us  [the longest x4 63.6 us: window_blocks(): pl.pallas_call(functools.partial(window_kernel, heads, len(arrays)), grid...]
    reshape x4 -> x0, local copies, waits for them, and re-layouts: 40.9 us -> none  [the longest x1 10.3 us: to_windows(): shaped.transpose(axes_order)]
    all_to_all x1, waiting for transfers between devices: 34.4 us -> 0.01 us  [on_device(): lax.all_to_all(buffer, ('lon', 'lat'), split_axis=0, concat_axis=0, tiled...]
    scatter-add x1 -> x0, other arithmetic: 30.8 us -> none  [on_device(): obs_field = jnp.zeros((levels * lat_rows * lon_cols, features), jnp.float...]
    ppermute x4 -> x8, waiting for transfers between devices: 29.1 us -> 4.82 us  [sent(): return lax.ppermute(block, ('lon', 'lat'), route)]
    gather x0 -> x6, local copies, waits for them, and re-layouts: none -> 19.5 us  [bias_tables(): base = (bias[:, order][:, :, order] * math.log2(math.e)).transpose(2, 0, 1)]
    scatter x2 -> x0, local copies, waits for them, and re-layouts: 18.8 us -> none  [the longest x1 9.99 us: on_device(): buffer = jnp.zeros((devices * capacity, payload.shape[1]), jnp.bfloat16)....]
    transpose x2 -> x0, local copies, waits for them, and re-layouts: 14.1 us -> none  [the longest x1 7.04 us: to_windows(): shaped.transpose(axes_order)]
  transfers between devices with their start and end apart: 6 -> 9, of which waited for: 4 -> 2; matrix products, arithmetic and copies ran while one was open for 12% -> 33% of each run, Pallas kernels for 0% -> 29%
where the time goes in v1:
time: 221 us; the launch traced here: 219 us
  Pallas kernels  115 us (52%)
  local copies, waits for them, and re-layouts  64 us (29%)
  starting transfers between devices  17.9 us (8%)
  other arithmetic  14.8 us (7%)
  waiting for transfers between devices  4.82 us (2%)
    pallas_call x4, Pallas kernels, window_blocks(): pl.pallas_call(functools.partial(window_kernel, heads, len(arrays)), grid...  63.6 us
    pallas_call x1, Pallas kernels, collect(): pl.pallas_call(functools.partial(collect_kernel, cap, levels, lat_rows),...  26.5 us
    gather x6, local copies, waits for them, and re-layouts, bias_tables(): base = (bias[:, order][:, :, order] * math.log2(math.e)).transpose(2, 0, 1)  19.5 us
    pallas_call x1, Pallas kernels, join(): pl.pallas_call(functools.partial(join_kernel, levels), grid=(units,), out...  15.7 us
    concatenate x17, local copies, waits for them, and re-layouts, lanes(): jnp.concatenate([main, tail, jnp.zeros((win, 128 - tail.shape[1]), t.dtyp...  14 us
    ppermute x8, starting transfers between devices, sent(): return lax.ppermute(block, ('lon', 'lat'), route)  10.4 us
    pallas_call x1, Pallas kernels, dispatch(): pl.pallas_call(functools.partial(dispatch_kernel, cap, devices), grid=(de...  9.33 us
    all_to_all x1, starting transfers between devices, on_device(): lax.all_to_all(buffer, ('lon', 'lat'), split_axis=0, concat_axis=0, tiled...  7.51 us
  transfers between devices with their start and end apart: 9, of which 2 were waited for; matrix products, arithmetic and copies ran while one was open for 33% of the time, Pallas kernels for 29%

profile of v1, /device:TPU:0, one launch (start us, length us, event | category | flops | bytes accessed | tf_op | source)
XLA Modules:
  0.0 219.3 jit_solution(11980437801287477651)
XLA Ops:
  2.1 1.4 convolution_convert_fusion
  4.2 1.6 maximum_maximum_fusion.payload_ref
  5.7 9.3 %shard_map.235 = bf16[32,200,128]{2,1,0:T(8,128)(2,1)} custom-call(s32[1]{0:T(128)S(6)} %copy.135.count_ref, s32[1,2048]{1,0:T(1,128)} %bitcast.63, bf16[2048,256]{1,0:T(8,128)(2,1)} %maximum_maximum_fusion.payload_ref), custom_call_target="tpu_custom_call" | custom-call | tf_op jit(solution)/shard_map/pallas_call | solution.py:226
  15.1 7.5 %all-to-all-start = ((bf16[32,200,128]{2,1,0:T(8,128)(2,1)}), bf16[32,200,128]{2,1,0:T(8,128)(2,1)S(1)}, u32[]{:S(2)}, u32[]{:S(2)}) async-start(bf16[32,200,128]{2,1,0:T(8,128)(2,1)} %shard_map.235), calls=%async_computation | async-start | bytes 3276800 | tf_op jit(solution)/shard_map/all_to_all | solution.py:402
  24.7 3.9 %gather_fusion.2 = f32[144,6,144]{2,0,1:T(8,128)} fusion(f32[6,144,144]{2,1,0:T(8,128)S(1)} %copy-done.2, s32[1024]{0:T(1024)S(1)} %pad_clamp_fusion), kind=kCustom, calls=%fused_computation.2 | custom fusion | bytes 995904 | tf_op jit(solution)/shard_map/gather | solution.py:157
  28.6 2.9 %copy.111 = f32[6,144,144]{1,0,2:T(8,128)} copy(f32[6,144,144]{2,1,0:T(8,128)} %bitcast.47) | data formatting | bytes 995328 | tf_op jit(solution)/shard_map/gather | solution.py:157
  31.5 3.0 %gather_fusion.3 = f32[144,6,144]{2,1,0:T(8,128)} fusion(f32[6,144,144]{1,0,2:T(8,128)} %copy.111, s32[1024]{0:T(1024)S(1)} %pad_clamp_fusion), kind=kCustom, calls=%fused_computation.3 | custom fusion | bytes 995904 | tf_op jit(solution)/shard_map/gather | solution.py:157
  34.5 1.4 broadcast_multiply_fusion
  36.8 3.9 %gather_fusion = f32[144,6,144]{2,0,1:T(8,128)} fusion(f32[6,144,144]{2,1,0:T(8,128)S(1)} %copy-done.2, s32[1024]{0:T(1024)S(1)} %pad_clamp_fusion.1), kind=kCustom, calls=%fused_computation | custom fusion | bytes 995904 | tf_op jit(solution)/shard_map/gather | solution.py:157
  40.7 2.9 %copy.96 = f32[6,144,144]{1,0,2:T(8,128)} copy(f32[6,144,144]{2,1,0:T(8,128)} %bitcast.48) | data formatting | bytes 995328 | tf_op jit(solution)/shard_map/gather | solution.py:157
  43.6 3.0 %gather_fusion.1 = f32[144,6,144]{2,1,0:T(8,128)} fusion(f32[6,144,144]{1,0,2:T(8,128)} %copy.96, s32[1024]{0:T(1024)S(1)} %pad_clamp_fusion.1), kind=kCustom, calls=%fused_computation.1 | custom fusion | bytes 995904 | tf_op jit(solution)/shard_map/gather | solution.py:157
  46.6 1.4 broadcast_multiply_fusion.1
  54.9 1.9 concatenate.184
  56.8 1.7 broadcast_in_dim.96
  58.6 1.9 concatenate.181
  70.4 26.5 %shard_map.236 = (bf16[12,3,144,192]{3,2,1,0:T(8,128)(2,1)}, bf16[12,3,72,192]{3,2,1,0:T(8,128)(2,1)}, bf16[12,3,72,192]{3,2,1,0:T(8,128)(2,1)}) custom-call(s32[4096]{0:T(1024)} %fusion.3.codes, bf16[32,200,128]{2,1,0:T(8,128)(2,1)} %copy-done.3, bf16[432,24,192]{2,1,0:T(8,128)(2,1)} %bitcast.44), custom_call_target="tpu_custom_call" | custom-call | tf_op jit(solution)/shard_map/pallas_call | solution.py:311
  97.0 2.2 collective-permute-start.3
  99.1 1.7 fusion.12
  109.0 2.6 %pad_maximum_fusion.1 = f32[4,144,896]{2,1,0:T(8,128)} fusion(f32[1,144,896]{2,1,0:T(8,128)} %get-tuple-element.21, f32[1,144,896]{2,1,0:T(8,128)S(1)} %copy-done.6, f32[1,144,896]{2,1,0:T(8,128)S(1)} %copy-done.5, f32[1,144,896]{2,1,0:T(8,128)S(1)} %copy-done.4), kind=kLoop, calls=%fused_computation.6 | loop fusion | flops 1548288 | bytes 4128768 | tf_op jit(solution)/shard_map/stack | solution.py:171
  111.9 1.5 pad_maximum_fusion
  115.1 3.3 %collective-permute-start.4 = (bf16[1,3,36,192]{3,2,1,0:T(8,128)(2,1)S(1)}, bf16[1,3,36,192]{3,2,1,0:T(8,128)(2,1)S(1)}, u32[]{:S(2)}, u32[]{:S(2)}) collective-permute-start(bf16[1,3,36,192]{3,2,1,0:T(8,128)(2,1)S(1)} %slice.117), channel_id=1, source_target_pairs={{0,31},{1,28},{2,29},{3,30},{4,3},{5,0},{6,1},{7,2},{8,7},{9,4},{1... | collective-permute-start | bytes 124424 | tf_op jit(solution)/shard_map/ppermute | solution.py:374
  120.3 2.3 %collective-permute-done.2 = bf16[1,3,36,192]{3,2,1,0:T(8,128)(2,1)S(1)} collective-permute-done((bf16[1,3,36,192]{3,2,1,0:T(8,128)(2,1)S(1)}, bf16[1,3,36,192]{3,2,1,0:T(8,128)(2,1)S(1)}, u32[]{:S(2)}, u32[]{:S(2)}) %collective-permute-start.2) | collective-permute-done | bytes 41504 | tf_op jit(solution)/shard_map/ppermute | solution.py:374
  122.6 1.5 dynamic_update_slice.16.refs_0_
  124.1 1.5 dynamic_update_slice.17.refs_1_
  125.6 29.1 %shard_map.240 = (bf16[12,3,72,192]{3,2,1,0:T(8,128)(2,1)}, bf16[12,3,72,192]{3,2,1,0:T(8,128)(2,1)}) custom-call(bf16[12,3,72,192]{3,2,1,0:T(8,128)(2,1)} %dynamic_update_slice.16.refs_0_, bf16[12,3,72,192]{3,2,1,0:T(8,128)(2,1)} %dynamic_update_slice.17.refs_1_, f32[2,2,144,896]{3,2,1,0:T(8,128)} %bitcast.49, f32[2,2,144,896]{3,2,1,0:T(8,128)} %bitcast.50, ...), custom_call_target="tpu_custom_call" | custom-call | flops 10368000000 | bytes 4147200 | tf_op jit(solution)/shard_map/pallas_call | solution.py:144
  154.7 15.8 %shard_map.237.refs_10_ = bf16[12,3,144,192]{3,2,1,0:T(8,128)(2,1)} custom-call(bf16[12,3,144,192]{3,2,1,0:T(8,128)(2,1)} %get-tuple-element.10.refs_0_, f32[2,2,144,896]{3,2,1,0:T(8,128)} %bitcast.38, f32[2,2,144,896]{3,2,1,0:T(8,128)} %bitcast.39, f32[1,192]{1,0:T(1,128)} %bitcast.65, bf16[192,192]{1,0:T(8,128)(2,1)} %get-tuple-element.26.refs_4_.refs_5_, ...), custom_call_target="tpu_custom_call" | custom-call | flops 5184000000 | bytes 2073600 | tf_op jit(solution)/shard_map/pallas_call | solution.py:144
  172.4 7.1 %shard_map.238.refs_10_ = bf16[12,3,144,192]{3,2,1,0:T(8,128)(2,1)} custom-call(bf16[2,3,144,192]{3,2,1,0:T(8,128)(2,1)} %maximum_maximum_fusion.3.refs_0_, f32[2,2,144,896]{3,2,1,0:T(8,128)} %bitcast.40, f32[2,2,144,896]{3,2,1,0:T(8,128)} %bitcast.41, f32[1,192]{1,0:T(1,128)} %bitcast.66, ...), custom_call_target="tpu_custom_call", output_to_operand_aliasing={{}: (10, {})} | custom-call | flops 1728000000 | bytes 691200 | tf_op jit(solution)/shard_map/pallas_call | solution.py:144
  180.4 11.5 %shard_map.239 = bf16[12,3,144,192]{3,2,1,0:T(8,128)(2,1)} custom-call(bf16[12,3,144,192]{3,2,1,0:T(8,128)(2,1)} %get-tuple-element.10.refs_0_, f32[2,2,144,896]{3,2,1,0:T(8,128)} %bitcast.42, f32[2,2,144,896]{3,2,1,0:T(8,128)} %bitcast.43, f32[1,192]{1,0:T(1,128)} %bitcast.67, ...), custom_call_target="tpu_custom_call", output_to_operand_aliasing={{}: (10, {})} | custom-call | flops 3456000000 | bytes 1382400 | tf_op jit(solution)/shard_map/pallas_call | solution.py:144
  194.3 3.3 %collective-permute-start.5 = (bf16[1,3,36,192]{3,2,1,0:T(8,128)(2,1)S(1)}, bf16[1,3,36,192]{3,2,1,0:T(8,128)(2,1)S(1)}, u32[]{:S(2)}, u32[]{:S(2)}) collective-permute-start(bf16[1,3,36,192]{3,2,1,0:T(8,128)(2,1)S(1)} %slice.126), channel_id=1, source_target_pairs={{0,1},{1,2},{2,3},{3,0},{4,5},{5,6},{6,7},{7,4},{8,9},{9,10},{10,1... | collective-permute-start | bytes 124424 | tf_op jit(solution)/shard_map/ppermute | solution.py:374
  198.3 2.5 %collective-permute-done.5 = bf16[1,3,36,192]{3,2,1,0:T(8,128)(2,1)S(1)} collective-permute-done((bf16[1,3,36,192]{3,2,1,0:T(8,128)(2,1)S(1)}, bf16[1,3,36,192]{3,2,1,0:T(8,128)(2,1)S(1)}, u32[]{:S(2)}, u32[]{:S(2)}) %collective-permute-start.5) | collective-permute-done | bytes 41504 | tf_op jit(solution)/shard_map/ppermute | solution.py:374
  200.8 1.5 dynamic_update_slice.18.right
  203.7 15.7 %shard_map.241 = bf16[6,72,24,192]{3,2,1,0:T(8,128)(2,1)} custom-call(bf16[12,3,144,192]{3,2,1,0:T(8,128)(2,1)} %constant_dynamic-update-slice_fusion.mid, bf16[12,3,72,192]{3,2,1,0:T(8,128)(2,1)} %dynamic_update_slice.18.right, bf16[12,3,72,192]{3,2,1,0:T(8,128)(2,1)} %copy-done.14), custom_call_target="tpu_custom_call" | custom-call | tf_op jit(solution)/shard_map/pallas_call | solution.py:360
  (163 shorter events, 40.6 us)
Async XLA Ops:
  0.0 2.1 copy-start
  15.1 7.6 %copy-start.29 = (f32[144,144]{0,1:T(8,128)S(1)}, f32[144,144]{0,1:T(8,128)}, u32[]{:S(2)}) copy-start(f32[144,144]{0,1:T(8,128)} %constant.93.clone) | copy-start | bytes 248836
  15.1 7.6 %copy-start.30 = (f32[144,144]{0,1:T(8,128)S(1)}, f32[144,144]{0,1:T(8,128)}, u32[]{:S(2)}) copy-start(f32[144,144]{0,1:T(8,128)} %constant.90.clone) | copy-start | bytes 248836
  15.1 7.6 %copy-start.31 = (f32[144,144]{0,1:T(8,128)S(1)}, f32[144,144]{0,1:T(8,128)}, u32[]{:S(2)}) copy-start(f32[144,144]{0,1:T(8,128)} %constant.88.clone) | copy-start | bytes 248836
  15.1 9.6 %copy-start.36 = (s32[144]{0:T(256)S(1)}, s32[144]{0:T(256)}, u32[]{:S(2)}) copy-start(s32[144]{0:T(256)} %constant.105) | copy-start | bytes 1732
  15.1 54.1 %all-to-all-start = ((bf16[32,200,128]{2,1,0:T(8,128)(2,1)}), bf16[32,200,128]{2,1,0:T(8,128)(2,1)S(1)}, u32[]{:S(2)}, u32[]{:S(2)}) async-start(bf16[32,200,128]{2,1,0:T(8,128)(2,1)} %shard_map.235), calls=%async_computation | async-start | bytes 3276800 | tf_op jit(solution)/shard_map/all_to_all | solution.py:402
  22.6 2.1 copy-start.2
  48.0 2.4 %copy-start.17 = (f32[144,128]{0,1:T(8,128)S(1)}, f32[144,128]{0,1:T(8,128)}, u32[]{:S(2)}) copy-start(f32[144,128]{0,1:T(8,128)} %slice.149) | copy-start | bytes 221188
  52.0 2.0 copy-start.21
  70.4 30.4 %copy-start.15 = (f32[144,144]{0,1:T(8,128)S(1)}, f32[144,144]{0,1:T(8,128)}, u32[]{:S(2)}) copy-start(f32[144,144]{0,1:T(8,128)} %get-tuple-element.30) | copy-start | bytes 248836
  97.0 4.9 %copy-start.33 = (f32[144,16]{0,1:T(8,128)S(1)}, f32[144,16]{0,1:T(8,128)}, u32[]{:S(2)}) copy-start(f32[144,16]{0,1:T(8,128)} %constant.98) | copy-start | bytes 27652
  97.0 5.8 %copy-start.22 = (bf16[768,192]{0,1:T(8,128)(2,1)S(1)}, bf16[768,192]{0,1:T(8,128)(2,1)}, u32[]{:S(2)}) copy-start(bf16[768,192]{0,1:T(8,128)(2,1)} %param.37) | copy-start | bytes 884740
  97.0 27.1 %collective-permute-start.3 = (bf16[12,3,72,192]{3,2,1,0:T(8,128)(2,1)}, bf16[12,3,72,192]{3,2,1,0:T(8,128)(2,1)}, u32[]{:S(2)}, u32[]{:S(2)}) collective-permute-start(bf16[12,3,72,192]{3,2,1,0:T(8,128)(2,1)} %get-tuple-element.12), channel_id=1, source_target_pairs={{0,28},{1,29},{2,30},{3,31},{4,0},{5,1},{6,2},{7,3},{8,4},{9,5},{1... | collective-permute-start | bytes 2985992 | tf_op jit(solution)/shard_map/ppermute | solution.py:374
  104.8 1.9 copy-start.32
  105.7 2.6 %copy-start.18 = (bf16[192,192]{0,1:T(8,128)(2,1)S(1)}, bf16[192,192]{0,1:T(8,128)(2,1)}, u32[]{:S(2)}) copy-start(bf16[192,192]{0,1:T(8,128)(2,1)} %copy.123) | copy-start | bytes 221188
  105.7 3.2 %copy-start.4 = (f32[1,144,896]{2,1,0:T(8,128)S(1)}, f32[1,144,896]{2,1,0:T(8,128)}, u32[]{:S(2)}) copy-start(f32[1,144,896]{2,1,0:T(8,128)} %get-tuple-element.36) | copy-start | bytes 1548292
  105.7 3.2 %copy-start.5 = (f32[1,144,896]{2,1,0:T(8,128)S(1)}, f32[1,144,896]{2,1,0:T(8,128)}, u32[]{:S(2)}) copy-start(f32[1,144,896]{2,1,0:T(8,128)} %get-tuple-element.19) | copy-start | bytes 1548292
  105.7 3.2 %copy-start.6 = (f32[1,144,896]{2,1,0:T(8,128)S(1)}, f32[1,144,896]{2,1,0:T(8,128)}, u32[]{:S(2)}) copy-start(f32[1,144,896]{2,1,0:T(8,128)} %get-tuple-element.20) | copy-start | bytes 1548292
  109.0 2.7 %copy-start.7 = (f32[1,144,768]{2,1,0:T(8,128)S(1)}, f32[1,144,768]{2,1,0:T(8,128)}, u32[]{:S(2)}) copy-start(f32[1,144,768]{2,1,0:T(8,128)} %concatenate.161) | copy-start | bytes 1327108
  109.0 2.7 %copy-start.11 = (f32[1,144,768]{2,1,0:T(8,128)S(1)}, f32[1,144,768]{2,1,0:T(8,128)}, u32[]{:S(2)}) copy-start(f32[1,144,768]{2,1,0:T(8,128)} %concatenate.168) | copy-start | bytes 1327108
  109.0 2.7 %copy-start.12 = (f32[1,144,768]{2,1,0:T(8,128)S(1)}, f32[1,144,768]{2,1,0:T(8,128)}, u32[]{:S(2)}) copy-start(f32[1,144,768]{2,1,0:T(8,128)} %concatenate.171) | copy-start | bytes 1327108
  109.0 2.7 %copy-start.13 = (f32[1,144,768]{2,1,0:T(8,128)S(1)}, f32[1,144,768]{2,1,0:T(8,128)}, u32[]{:S(2)}) copy-start(f32[1,144,768]{2,1,0:T(8,128)} %concatenate.165) | copy-start | bytes 1327108
  109.0 2.7 %copy-start.27 = (f32[1,144,96]{2,1,0:T(8,128)S(1)}, f32[1,144,96]{2,1,0:T(8,128)}, u32[]{:S(2)}) copy-start(f32[1,144,96]{2,1,0:T(8,128)} %copy.105) | copy-start | bytes 165892
  109.0 2.7 %copy-start.28 = (f32[1,144,96]{2,1,0:T(8,128)S(1)}, f32[1,144,96]{2,1,0:T(8,128)}, u32[]{:S(2)}) copy-start(f32[1,144,96]{2,1,0:T(8,128)} %copy.100) | copy-start | bytes 165892
  115.1 9.0 %collective-permute-start.4 = (bf16[1,3,36,192]{3,2,1,0:T(8,128)(2,1)S(1)}, bf16[1,3,36,192]{3,2,1,0:T(8,128)(2,1)S(1)}, u32[]{:S(2)}, u32[]{:S(2)}) collective-permute-start(bf16[1,3,36,192]{3,2,1,0:T(8,128)(2,1)S(1)} %slice.117), channel_id=1, source_target_pairs={{0,31},{1,28},{2,29},{3,30},{4,3},{5,0},{6,1},{7,2},{8,7},{9,4},{1... | collective-permute-start | bytes 124424 | tf_op jit(solution)/shard_map/ppermute | solution.py:374
  118.4 4.2 %collective-permute-start.2 = (bf16[1,3,36,192]{3,2,1,0:T(8,128)(2,1)S(1)}, bf16[1,3,36,192]{3,2,1,0:T(8,128)(2,1)S(1)}, u32[]{:S(2)}, u32[]{:S(2)}) collective-permute-start(bf16[1,3,36,192]{3,2,1,0:T(8,128)(2,1)S(1)} %slice.116), channel_id=1, source_target_pairs={{0,3},{1,0},{2,1},{3,2},{4,7},{5,4},{6,5},{7,6},{8,11},{9,8},{10,9... | collective-permute-start | bytes 124424 | tf_op jit(solution)/shard_map/ppermute | solution.py:374
  119.8 51.7 %collective-permute-start = (bf16[1,3,72,192]{3,2,1,0:T(8,128)(2,1)S(1)}, bf16[1,3,72,192]{3,2,1,0:T(8,128)(2,1)S(1)}, u32[]{:S(2)}, u32[]{:S(2)}) collective-permute-start(bf16[1,3,72,192]{3,2,1,0:T(8,128)(2,1)S(1)} %get-tuple-element.18), channel_id=1, source_target_pairs={{0,3},{1,0},{2,1},{3,2},{4,7},{5,4},{6,5},{7,6},{8,11},{9,8},{10,9... | collective-permute-start | bytes 248840 | tf_op jit(solution)/shard_map/ppermute | solution.py:374
  154.7 47.6 %collective-permute-start.6 = (bf16[12,3,72,192]{3,2,1,0:T(8,128)(2,1)}, bf16[12,3,72,192]{3,2,1,0:T(8,128)(2,1)S(1)}, u32[]{:S(2)}, u32[]{:S(2)}) collective-permute-start(bf16[12,3,72,192]{3,2,1,0:T(8,128)(2,1)} %get-tuple-element.14), channel_id=1, source_target_pairs={{0,4},{1,5},{2,6},{3,7},{4,8},{5,9},{6,10},{7,11},{8,12},{9,13},{1... | collective-permute-start | bytes 2985992 | tf_op jit(solution)/shard_map/ppermute | solution.py:374
  180.4 17.3 %collective-permute-start.1 = (bf16[1,3,72,192]{3,2,1,0:T(8,128)(2,1)S(1)}, bf16[1,3,72,192]{3,2,1,0:T(8,128)(2,1)S(1)}, u32[]{:S(2)}, u32[]{:S(2)}) collective-permute-start(bf16[1,3,72,192]{3,2,1,0:T(8,128)(2,1)S(1)} %slice.144), channel_id=1, source_target_pairs={{0,1},{1,2},{2,3},{3,0},{4,5},{5,6},{6,7},{7,4},{8,9},{9,10},{10,1... | collective-permute-start | bytes 248840 | tf_op jit(solution)/shard_map/ppermute | solution.py:374
  193.7 8.6 %collective-permute-start.7 = (bf16[1,3,36,192]{3,2,1,0:T(8,128)(2,1)S(1)}, bf16[1,3,36,192]{3,2,1,0:T(8,128)(2,1)S(1)}, u32[]{:S(2)}, u32[]{:S(2)}) collective-permute-start(bf16[1,3,36,192]{3,2,1,0:T(8,128)(2,1)S(1)} %slice.127), channel_id=1, source_target_pairs={{0,5},{1,6},{2,7},{3,4},{4,9},{5,10},{6,11},{7,8},{8,13},{9,14},{1... | collective-permute-start | bytes 124424 | tf_op jit(solution)/shard_map/ppermute | solution.py:374
  194.3 6.5 %collective-permute-start.5 = (bf16[1,3,36,192]{3,2,1,0:T(8,128)(2,1)S(1)}, bf16[1,3,36,192]{3,2,1,0:T(8,128)(2,1)S(1)}, u32[]{:S(2)}, u32[]{:S(2)}) collective-permute-start(bf16[1,3,36,192]{3,2,1,0:T(8,128)(2,1)S(1)} %slice.126), channel_id=1, source_target_pairs={{0,1},{1,2},{2,3},{3,0},{4,5},{5,6},{6,7},{7,4},{8,9},{9,10},{10,1... | collective-permute-start | bytes 124424 | tf_op jit(solution)/shard_map/ppermute | solution.py:374
  203.7 15.7 %copy-start.1 = (bf16[2048,256]{1,0:T(8,128)(2,1)S(1)}, bf16[2048,256]{1,0:T(8,128)(2,1)}, u32[]{:S(2)}) copy-start(bf16[2048,256]{1,0:T(8,128)(2,1)} %param.26) | copy-start | bytes 3145732
  (14 other events, 19.8 us)
